TPU v7x, 32 devices: a whole 2x2x4 slice. The times are simulated.
32 devices in a mesh: grp: 2 (over y), blk: 4 (over z), bulk: 4 (over x, core).
Axes of the slice: x: 2, y: 2, z: 4, core: 2. Of those that a mesh axis runs over, the one named last changes fastest.
Arguments:
- tokens: bfloat16 [80, 8192], P(('grp', 'blk'), 'bulk'), parts along dimension 0, may hold values from -6 to 6
- cotangent: bfloat16 [80, 8192], P(('grp', 'blk'), 'bulk'), parts along dimension 0, may hold values from -1.5 to 1.5
- gate_weight: bfloat16 [8192, 26624], P('bulk', 'blk'), may hold values from -0.0625 to 0.0625
- up_weight: bfloat16 [8192, 26624], P('bulk', 'blk'), may hold values from -0.0625 to 0.0625
- down_weight: bfloat16 [26624, 8192], P('blk', 'bulk'), may hold values from -0.0390625 to 0.0390625
Outputs:
- mixed: bfloat16 [80, 8192], P(('grp', 'blk'), 'bulk'), parts along dimension 0
- grad_input: bfloat16 [80, 8192], P(('grp', 'blk'), 'bulk'), parts along dimension 0
There are 2 independent parts, one for each index of `grp`. A program takes and returns all parts, laid end to end along the dimension named above; an argument that names none is the same for every part. Nothing has to cross between parts.
All inputs are finite; a program needn't handle non-finite values.
Results may differ from a plain program's by a relative error of at most 0.0049.
Values may be sent and summed in bfloat16 or wider, within the bound.
A program may use at most 192 MiB of HBM per device.

v0:
```python
import jax
import jax.numpy as jnp
from jax import lax
from jax.sharding import PartitionSpec as P


def per_device(tokens, cotangent, gate_weight, up_weight, down_weight):
    token_all, cot_all = (
        lax.all_gather(tokens, "blk", axis=0, tiled=True),
        lax.all_gather(cotangent, "blk", axis=0, tiled=True),
    )
    width = gate_weight.shape[1]
    paired = jnp.concatenate([gate_weight, up_weight], axis=1)
    block = token_all
    gate_up = lax.psum_scatter(
        jnp.dot(block, paired, preferred_element_type=jnp.float32),
        "bulk",
        scatter_dimension=0,
        tiled=True,
    )
    gate = gate_up[:, :width]
    upward = gate_up[:, width:]
    sigma = jax.nn.sigmoid(gate)
    hidden = (gate * sigma * upward).astype(jnp.bfloat16)
    hidden_all = lax.all_gather(hidden, "bulk", axis=0, tiled=True)
    block = hidden_all
    mixed = lax.psum_scatter(
        jnp.dot(block, down_weight, preferred_element_type=jnp.float32),
        "blk",
        scatter_dimension=0,
        tiled=True,
    ).astype(jnp.bfloat16)
    block = cot_all
    back = lax.psum_scatter(
        lax.dot_general(
            block, down_weight, (((1,), (1,)), ((), ())), preferred_element_type=jnp.float32
        ),
        "bulk",
        scatter_dimension=0,
        tiled=True,
    )
    d_up = (back * gate * sigma).astype(jnp.bfloat16)
    d_gate = (back * upward * sigma * (1.0 + gate * (1.0 - sigma))).astype(jnp.bfloat16)
    grads_local = jnp.concatenate([d_gate, d_up], axis=1)
    grads_all = lax.all_gather(grads_local, "bulk", axis=0, tiled=True)
    block = grads_all
    grad_input = lax.psum_scatter(
        lax.dot_general(
            block, paired, (((1,), (1,)), ((), ())), preferred_element_type=jnp.float32
        ),
        "blk",
        scatter_dimension=0,
        tiled=True,
    ).astype(jnp.bfloat16)
    return (mixed, grad_input)


def solution(mesh):
    return jax.shard_map(
        per_device,
        mesh=mesh,
        in_specs=(
            P(("grp", "blk"), "bulk"),
            P(("grp", "blk"), "bulk"),
            P("bulk", "blk"),
            P("bulk", "blk"),
            P("blk", "bulk"),
        ),
        out_specs=(P(("grp", "blk"), "bulk"), P(("grp", "blk"), "bulk")),
        check_vma=False,
    )
```

profile of v0, /device:TPU:0, one launch (start us, length us, event | category | flops | bytes accessed | tf_op | source)
XLA Modules:
  0.0 269.0 jit_solution(2728264743056934311)
XLA Ops:
  7.2 0.0 all-reduce.9.cloned.1.call-start
  7.2 19.2 %constant_dynamic-update-slice_fusion.1 = bf16[2048,13312]{1,0:T(8,128)(2,1)} fusion(bf16[2048,6656]{1,0:T(8,128)(2,1)} %param.7), kind=kLoop, calls=%fused_computation.10 | loop fusion | bytes 54525952
  26.5 15.7 %all-gather = bf16[4,10,2048]{2,1,0:T(8,128)(2,1)S(1)} all-gather(bf16[1,10,2048]{2,1,0:T(8,128)(2,1)S(1)} %bitcast.18), channel_id=1, replica_groups=mesh['grp'=2,'blk'=4,'bulk'=4] {'blk'}, dimensions={0}, use_global_device_ids=true | all-gather | bytes 204800 | tf_op jit(solution)/shard_map/all_gather | solution.py:9
  42.1 0.1 reshape.5
  42.2 14.4 %all-gather.2 = bf16[4,10,2048]{2,1,0:T(8,128)(2,1)S(1)} all-gather(bf16[1,10,2048]{2,1,0:T(8,128)(2,1)S(1)} %bitcast.19), channel_id=1, replica_groups=mesh['grp'=2,'blk'=4,'bulk'=4] {'blk'}, dimensions={0}, use_global_device_ids=true | all-gather | bytes 204800 | tf_op jit(solution)/shard_map/all_gather | solution.py:10
  56.7 0.1 reshape.9
  56.7 19.4 %constant_dynamic-update-slice_fusion = bf16[2048,13312]{1,0:T(8,128)(2,1)} fusion(bf16[2048,13312]{1,0:T(8,128)(2,1)} %constant_dynamic-update-slice_fusion.1, bf16[2048,6656]{1,0:T(8,128)(2,1)} %param.8), kind=kLoop, calls=%fused_computation.9 | loop fusion | bytes 54525952 | tf_op jit(solution)/shard_map/concatenate | solution.py:13
  76.1 20.5 %convolution_bitcast_fusion = f32[40,13312]{1,0:T(8,128)} fusion(bf16[2048,13312]{1,0:T(8,128)(2,1)} %constant_dynamic-update-slice_fusion, bf16[40,2048]{1,0:T(8,128)(2,1)S(1)} %reshape.5), kind=kOutput, calls=%fused_computation | convolution fusion | flops 2181038080 | bytes 56819712 | tf_op jit(solution)/shard_map/dot_general | solution.py:16
  96.6 14.3 %fusion.2 = f32[40,6656]{1,0:T(8,128)} fusion(bf16[40,2048]{1,0:T(8,128)(2,1)S(1)} %reshape.9, bf16[6656,2048]{1,0:T(8,128)(2,1)} %param.9), kind=kOutput, calls=%fused_computation.12 | convolution fusion | flops 1090519040 | bytes 28491776 | tf_op jit(solution)/shard_map/dot_general | solution.py:35
  111.0 0.0 all-gather.6.cloned.1.call-start
  111.0 0.6 dynamic-slice
  111.6 0.6 dynamic-slice.2
  113.5 68.1 %all-reduce.9.cloned.1.call-done = (f32[40,13312]{1,0:T(8,128)}, f32[40,6656]{1,0:T(8,128)}) async-done(((f32[40,13312]{1,0:T(8,128)}, f32[40,6656]{1,0:T(8,128)}), (f32[40,13312]{1,0:T(8,128)}, f32[40,6656]{1,0:T(8,128)})) %all-reduce.9.cloned.1.call-update) | async-done | bytes 3194896
  181.6 1.8 multiply_convert_fusion.1
  183.4 0.8 maximum_bitcast_fusion
  184.1 0.0 all-gather.6.cloned.1.call-update
  184.2 8.6 %all-gather.1 = bf16[4,10,6656]{2,1,0:T(8,128)(2,1)S(1)} all-gather(bf16[1,10,6656]{2,1,0:T(8,128)(2,1)S(1)} %get-tuple-element.8), channel_id=1, replica_groups=mesh['grp'=2,'blk'=4,'bulk'=4] {'bulk'}, dimensions={0}, use_global_device_ids=true | all-gather | bytes 665600 | tf_op jit(solution)/shard_map/all_gather | solution.py:25
  192.8 0.2 reshape.7
  193.0 11.3 %fusion.1 = f32[40,2048]{1,0:T(8,128)S(1)} fusion(bf16[40,6656]{1,0:T(8,128)(2,1)S(1)} %reshape.7, bf16[6656,2048]{1,0:T(8,128)(2,1)} %param.9), kind=kOutput, calls=%fused_computation.11 | convolution fusion | flops 1090519040 | bytes 28123136 | tf_op jit(solution)/shard_map/dot_general | solution.py:28
  204.3 0.4 all-gather.6.cloned.1.call-done
  204.7 1.9 reshape.11
  206.6 22.5 %fusion.3 = f32[40,2048]{1,0:T(8,128)S(1)} fusion(bf16[40,13312]{1,0:T(8,128)(2,1)S(1)} %reshape.11, bf16[2048,13312]{1,0:T(8,128)(2,1)} %constant_dynamic-update-slice_fusion), kind=kOutput, calls=%fused_computation.13 | convolution fusion | flops 2181038080 | bytes 55918592 | tf_op jit(solution)/shard_map/dot_general | solution.py:48
  229.1 32.4 %all-reduce.10 = (bf16[40,2048]{1,0:T(8,128)(2,1)S(1)}, bf16[40,2048]{1,0:T(8,128)(2,1)S(1)}) all-reduce(f32[40,2048]{1,0:T(8,128)S(1)} %fusion.1, f32[40,2048]{1,0:T(8,128)S(1)} %fusion.3), channel_id=3, replica_groups=mesh['grp'=2,'blk'=4,'bulk'=4] {'blk'}, use_global_device_ids=true, to_apply=%region_1.0.clone | all-reduce | flops 163840 | bytes 983040
  261.5 0.7 dynamic-slice_convert_fusion
  (9 shorter events, 0.0 us)
Async XLA Ops:
  7.2 19.3 %copy-start = (bf16[10,2048]{1,0:T(8,128)(2,1)S(1)}, bf16[10,2048]{1,0:T(8,128)(2,1)}, u32[]{:S(2)}) copy-start(bf16[10,2048]{1,0:T(8,128)(2,1)} %param.5) | copy-start | bytes 122884
  7.2 35.0 %copy-start.1 = (bf16[10,2048]{1,0:T(8,128)(2,1)S(1)}, bf16[10,2048]{1,0:T(8,128)(2,1)}, u32[]{:S(2)}) copy-start(bf16[10,2048]{1,0:T(8,128)(2,1)} %param.6) | copy-start | bytes 122884
  7.2 174.4 %all-reduce.9.cloned.1.call-start = ((), (), s32[]{:S(2)}) async-start(), calls=%async_computation.1 | async-start | bytes 6389760
  96.6 14.4 %copy-start.3 = (u32[32]{0:T(128)S(1)}, u32[32]{0:T(128)}, u32[]{:S(2)}) copy-start(u32[32]{0:T(128)} %constant.6) | copy-start | bytes 388
  96.6 15.0 %copy-start.2 = (u32[32]{0:T(128)S(1)}, u32[32]{0:T(128)}, u32[]{:S(2)}) copy-start(u32[32]{0:T(128)} %constant.10) | copy-start | bytes 388
  111.0 93.7 %all-gather.6.cloned.1.call-start = ((), (), s32[]{:S(2)}) async-start(), calls=%async_computation | async-start | bytes 2129920 | tf_op jit(solution)/shard_map/all_gather | solution.py:45
Sparse Core Ops, SparseCore 0:
  111.1 70.4 all-reduce.8
  184.3 20.3 all-gather.5
where the time goes:
time: 269 us
  blocking collectives  71.2 us (26%)
  matrix products  68.6 us (26%)
  waiting for transfers between devices  68.5 us (25%)
  local copies, waits for them, and re-layouts  42.7 us (16%)
  between operations  15.4 us (6%)
    unnamed x3, waiting for transfers between devices  68.1 us
    unnamed x1, blocking collectives  32.4 us
    unnamed x15, local copies, waits for them, and re-layouts  22.6 us
    dot_general x1, matrix products, per_device(): lax.dot_general(block, paired, (((1,), (1,)), ((), ())), preferred_elemen...  22.5 us
    dot_general x1, matrix products, per_device(): jnp.dot(block, paired, preferred_element_type=jnp.float32)  20.5 us
    concatenate x1, local copies, waits for them, and re-layouts, per_device(): paired = jnp.concatenate([gate_weight, up_weight], axis=1)  19.4 us
    all_gather x1, blocking collectives, per_device(): lax.all_gather(tokens, 'blk', axis=0, tiled=True)  15.7 us
    all_gather x1, blocking collectives, per_device(): lax.all_gather(cotangent, 'blk', axis=0, tiled=True)  14.4 us
  transfers between devices with their start and end apart: 2, of which 2 were waited for; matrix products, arithmetic and copies ran while one was open for 5% of the time, Pallas kernels for 0%

commit v1 on v0

v1 whole, which is shorter than its diff:
```python
import functools

import jax
import jax.numpy as jnp
from jax import lax
from jax.experimental import pallas as pl
from jax.experimental.pallas import tpu as pltpu
from jax.sharding import PartitionSpec as P

MESH = pl.DeviceIdType.MESH
BF = jnp.bfloat16
F32 = jnp.float32

S1 = 1
S2 = 3
S3 = 4
S4 = 7
S5 = 8
S6 = 11
AHEAD = 8
RING = 3
NT = (((1,), (1,)), ((), ()))


def kernel(nb, nu, n, fc, tok_in, cot_in, wg_hbm, wu_hbm, wd_hbm, mixed_out, grad_out,
           wg, wu, wd, tok_g, cot_g, tok, cot, part, pair, far, act, mixed, grad, stage, zbuf,
           g_sem, u_sem, d_sem, tk_send, tk_recv, p_send, p_recv, f_send, f_recv,
           a_send, a_recv, fw_send, z_send, z_recv):
    b_me = lax.axis_index("blk")
    u_me = lax.axis_index("bulk")
    x_me, k_me = u_me // 2, u_me % 2
    chips = nu // 2
    rows = tok_in.shape[0]
    dh = grad.shape[2]
    partner = x_me * 2 + (1 - k_me)

    def load_gu(c):
        cols = pl.ds(pl.multiple_of(c * fc, fc), fc)
        return (pltpu.make_async_copy(wg_hbm.at[:, cols], wg.at[c], g_sem.at[c]),
                pltpu.make_async_copy(wu_hbm.at[:, cols], wu.at[c], u_sem.at[c]))

    def load_d(m):
        c = m % n
        slot = m % RING
        return pltpu.make_async_copy(
            wd_hbm.at[pl.ds(pl.multiple_of(c * fc, fc), fc), :], wd.at[slot], d_sem.at[slot])

    ahead = min(AHEAD, n)
    for c in range(ahead):
        for cp in load_gu(c):
            cp.start()
        if c < RING:
            load_d(c).start()

    barrier = pltpu.get_barrier_semaphore()
    for d in range(1, nb):
        pl.semaphore_signal(barrier, inc=1, device_id={"blk": (b_me + d) % nb}, device_id_type=MESH)
    for d in range(1, nu):
        pl.semaphore_signal(barrier, inc=1, device_id={"bulk": (u_me + d) % nu}, device_id_type=MESH)
    pl.semaphore_wait(barrier, nb + nu - 2)

    def rcopy(src, dst, ss, rs, where):
        return pltpu.make_async_remote_copy(
            src_ref=src, dst_ref=dst, send_sem=ss, recv_sem=rs, device_id=where, device_id_type=MESH)

    def tok_copy(w, d):
        src, dst = (tok_in, tok_g) if w == 0 else (cot_in, cot_g)
        return rcopy(src, dst.at[d - 1], tk_send.at[w, d - 1], tk_recv.at[w, d - 1],
                     {"blk": (b_me + d) % nb})

    for w in range(2):
        for d in range(1, nb):
            tok_copy(w, d).start()
    for src, got, dst, which in ((tok_in, tok_g, tok, 0), (cot_in, cot_g, cot, 1)):
        for d in range(1, nb):
            tok_copy(which, d).wait_recv()
        for h in range(2):
            cols = pl.ds(h * dh, dh)
            for b in range(nb):
                slot = (b_me - b + nb) % nb
                other = got[jnp.maximum(slot - 1, 0), :, cols].astype(F32)
                own = src[:, cols].astype(F32)
                mixed[h, pl.ds(b * rows, rows), :] = jnp.where(slot == 0, own, other)
        for h in range(2):
            dst[:, h * dh:(h + 1) * dh] = mixed[h].astype(BF)

    def owner(c):
        o = c % nu
        return o, o // 2, o % 2

    def pair_copy(c):
        return rcopy(part.at[c], pair.at[c // 2], p_send.at[c], p_recv.at[c // 2], {"bulk": partner})

    def far_copy(c):
        o, ox, ok = owner(c)
        slot = (x_me - ox + chips - 1 + chips) % chips
        return rcopy(pair.at[c // 2], far.at[c // nu, slot], f_send.at[c // 2],
                     f_recv.at[c // nu, slot], {"bulk": o})

    def far_wait(c, slot):
        rcopy(pair.at[c // 2], far.at[c // nu, slot], f_send.at[c // 2],
              f_recv.at[c // nu, slot], {"bulk": partner}).wait_recv()

    def act_copy(c, d):
        to = partner if d == 0 else ((x_me + d) % chips) * 2 + k_me
        return rcopy(act.at[c], act.at[c], a_send.at[c // nu, d], a_recv.at[c], {"bulk": to})

    def forward(c):
        return rcopy(act.at[c], act.at[c], fw_send.at[c // 2], a_recv.at[c], {"bulk": partner})

    def valid(c):
        return jnp.logical_and(c >= 0, c < n)

    def stages(i):
        c1 = i - S1

        @pl.when(jnp.logical_and(valid(c1), owner(c1 + nu)[2] != k_me))
        def _():
            pair_copy(c1).start()

        c3 = i - S3
        o3 = owner(c3 + nu)

        @pl.when(jnp.logical_and(valid(c3), jnp.logical_and(o3[2] == k_me, o3[1] != x_me)))
        def _():
            far_copy(c3).start()

        c5 = i - S5

        @pl.when(jnp.logical_and(valid(c5), owner(c5 + nu)[0] == u_me))
        def _():
            for d in range(chips):
                act_copy(c5, d).start()

        c6 = i - S6
        o6 = owner(c6 + nu)

        @pl.when(jnp.logical_and(valid(c6), jnp.logical_and(o6[2] == k_me, o6[1] != x_me)))
        def _():
            forward(c6).wait_recv()
            forward(c6).start()

        c2 = i - S2
        o2 = owner(c2 + nu)

        @pl.when(jnp.logical_and(valid(c2), o2[2] == k_me))
        def _():
            pair_copy(c2).wait_recv()

            @pl.when(o2[1] != x_me)
            def _():
                for j in range(3):
                    pair[c2 // 2, j] = (
                        part[c2, j].astype(F32) + pair[c2 // 2, j].astype(F32)).astype(BF)

        c4 = i - S4

        @pl.when(jnp.logical_and(valid(c4), owner(c4 + nu)[0] == u_me))
        def _():
            for slot in range(chips - 1):
                far_wait(c4, slot)

            def total(j):
                s = part[c4, j].astype(F32) + pair[c4 // 2, j].astype(F32)
                for slot in range(chips - 1):
                    s = s + far[c4 // nu, slot, j].astype(F32)
                return s

            gate, upward, back = total(0), total(1), total(2)
            sigma = 1.0 / (1.0 + jnp.exp(-gate))
            act[c4, 0] = (gate * sigma * upward).astype(BF)
            act[c4, 1] = (back * upward * sigma * (1.0 + gate * (1.0 - sigma))).astype(BF)
            act[c4, 2] = (back * gate * sigma).astype(BF)

    def first(i, _):
        stages(i)

        @pl.when(i + ahead < n)
        def _():
            for cp in load_gu(i + ahead):
                cp.start()

        for cp in load_gu(i):
            cp.wait()
        part[i, 0] = jnp.dot(tok[...], wg[i], preferred_element_type=F32).astype(BF)
        part[i, 1] = jnp.dot(tok[...], wu[i], preferred_element_type=F32).astype(BF)
        load_d(i).wait()
        part[i, 2] = lax.dot_general(
            cot[...], wd[i % RING], NT, preferred_element_type=F32).astype(BF)
        load_d(i + RING).start()
        return 0

    lax.fori_loop(0, n, first, 0)

    mixed[...] = jnp.zeros_like(mixed)
    grad[...] = jnp.zeros_like(grad)

    def second(j, _):
        i = j + n
        stages(i)

        @pl.when(owner(j)[2] != k_me)
        def _():
            forward(j).wait_recv()

        load_d(i).wait()
        for h in range(2):
            mixed[h] += jnp.dot(
                act[j, 0], wd[i % RING, :, h * dh:(h + 1) * dh], preferred_element_type=F32)

        @pl.when(i + RING < 2 * n)
        def _():
            load_d(i + RING).start()

        return 0

    lax.fori_loop(0, n, second, 0)

    def z_stage(q):
        acc = mixed if q < 2 else grad
        for b in range(nb):
            stage[q, b] = acc[q % 2, b * rows:(b + 1) * rows, :].astype(BF)

    def z_copy(q, d):
        to = (b_me + d) % nb
        return rcopy(stage.at[q, to], zbuf.at[q, d - 1], z_send.at[q, d - 1], z_recv.at[q, d - 1],
                     {"blk": to})

    def z_send_all(q):
        for d in range(1, nb):
            z_copy(q, d).start()

    def z_finish(q):
        acc, out = (mixed, mixed_out) if q < 2 else (grad, grad_out)
        h = q % 2
        s = jnp.zeros((rows, dh), F32)
        for b in range(nb):
            s = s + jnp.where(b == b_me, acc[h, b * rows:(b + 1) * rows, :], 0.0)
        for d in range(1, nb):
            z_copy(q, d).wait_recv()
            s = s + zbuf[q, d - 1].astype(F32)
        out[:, h * dh:(h + 1) * dh] = s.astype(BF)

    z_stage(0)
    z_stage(1)
    for h in range(2):
        def third(c, _, h=h):
            @pl.when(c == 1)
            def _():
                for q in ((0, 1) if h == 0 else (2,)):
                    z_send_all(q)

            grad[h] += (
                lax.dot_general(act[c, 1], wg[c, h * dh:(h + 1) * dh, :], NT,
                                preferred_element_type=F32)
                + lax.dot_general(act[c, 2], wu[c, h * dh:(h + 1) * dh, :], NT,
                                  preferred_element_type=F32))
            return 0

        lax.fori_loop(0, n, third, 0)
        z_stage(2 + h)
    z_finish(0)
    z_send_all(3)
    z_finish(1)
    z_finish(2)

    for d in range(1, nb):
        for w in range(2):
            tok_copy(w, d).wait_send()

    def drain(c, _):
        o, ox, ok = owner(c)

        @pl.when(ok != k_me)
        def _():
            pair_copy(c).wait_send()

        @pl.when(jnp.logical_and(ok == k_me, ox != x_me))
        def _():
            far_copy(c).wait_send()
            forward(c).wait_send()

        @pl.when(o == u_me)
        def _():
            for d in range(chips):
                act_copy(c, d).wait_send()

        return 0

    lax.fori_loop(0, n, drain, 0)
    z_finish(3)
    for q in range(4):
        for d in range(1, nb):
            z_copy(q, d).wait_send()


def per_device(nb, nu, tokens, cotangent, gate_weight, up_weight, down_weight):
    rows, depth = tokens.shape
    width = gate_weight.shape[1]
    fc = next(w for w in (256, 128) if width % w == 0)
    n = width // fc
    assert n >= S6 and depth % 256 == 0 and nu % 2 == 0
    t = rows * nb
    dh = depth // 2
    owned = pl.cdiv(n, nu)
    halfn = pl.cdiv(n, 2)
    chips = nu // 2
    dma = pltpu.SemaphoreType.DMA
    vm = pltpu.VMEM
    out = jax.ShapeDtypeStruct((rows, depth), BF)
    return pl.pallas_call(
        functools.partial(kernel, nb, nu, n, fc),
        out_shape=(out, out),
        in_specs=[pl.BlockSpec(memory_space=pltpu.VMEM)] * 2 + [pl.BlockSpec(memory_space=pl.ANY)] * 3,
        out_specs=(pl.BlockSpec(memory_space=pltpu.VMEM),) * 2,
        scratch_shapes=[
            vm((n, depth, fc), BF), vm((n, depth, fc), BF), vm((RING, fc, depth), BF),
            vm((nb - 1, rows, depth), BF), vm((nb - 1, rows, depth), BF),
            vm((t, depth), BF), vm((t, depth), BF),
            vm((n, 3, t, fc), BF), vm((halfn, 3, t, fc), BF), vm((owned, chips - 1, 3, t, fc), BF),
            vm((n, 3, t, fc), BF),
            vm((2, t, dh), F32), vm((2, t, dh), F32),
            vm((4, nb, rows, dh), BF), vm((4, nb - 1, rows, dh), BF),
            dma((n,)), dma((n,)), dma((RING,)),
            dma((2, nb - 1)), dma((2, nb - 1)),
            dma((n,)), dma((halfn,)), dma((halfn,)), dma((owned, chips - 1)),
            dma((owned, chips)), dma((n,)), dma((halfn,)),
            dma((4, nb - 1)), dma((4, nb - 1)),
        ],
        compiler_params=pltpu.CompilerParams(
            collective_id=0, has_side_effects=True, vmem_limit_bytes=67043328),
    )(tokens, cotangent, gate_weight, up_weight, down_weight)


def solution(mesh):
    return jax.shard_map(
        functools.partial(per_device, mesh.shape["blk"], mesh.shape["bulk"]),
        mesh=mesh,
        in_specs=(
            P(("grp", "blk"), "bulk"),
            P(("grp", "blk"), "bulk"),
            P("bulk", "blk"),
            P("bulk", "blk"),
            P("blk", "bulk"),
        ),
        out_specs=(P(("grp", "blk"), "bulk"), P(("grp", "blk"), "bulk")),
        check_vma=False,
    )
```

time: 269 us -> 97.3 us (0.36)
  Pallas kernels: 0 us -> 93.3 us
  blocking collectives: 71.2 us -> 0 us
  matrix products: 68.6 us -> 0 us
  waiting for transfers between devices: 68.5 us -> 0 us
  local copies, waits for them, and re-layouts: 42.7 us -> 2.95 us
  between operations: 15.4 us -> 0.64 us
    pallas_call x0 -> x1, Pallas kernels: none -> 93.3 us  [per_device(): pl.pallas_call(functools.partial(kernel, nb, nu, n, fc), out_shape=(out,...]
    dot_general x4 -> x0, matrix products: 68.6 us -> none  [the longest x1 22.5 us: per_device(): lax.dot_general(block, paired, (((1,), (1,)), ((), ())), preferred_elemen...]
    unnamed x3 -> x0, waiting for transfers between devices: 68.1 us -> none
    all_gather x3 -> x0, blocking collectives: 38.7 us -> none  [the longest x1 15.7 us: per_device(): lax.all_gather(tokens, 'blk', axis=0, tiled=True)]
    unnamed x1 -> x0, blocking collectives: 32.4 us -> none
    unnamed x15 -> x2, local copies, waits for them, and re-layouts: 22.6 us -> 2.95 us
    concatenate x1 -> x0, local copies, waits for them, and re-layouts: 19.4 us -> none  [per_device(): paired = jnp.concatenate([gate_weight, up_weight], axis=1)]
  transfers between devices with their start and end apart: 2 -> 0, of which waited for: 2 -> 0; matrix products, arithmetic and copies ran while one was open for 5% -> 0% of each run, Pallas kernels for 0% -> 0%
where the time goes in v1:
time: 97.3 us; the launch traced here: 96.9 us
  Pallas kernels  93.3 us (96%)
  local copies, waits for them, and re-layouts  2.95 us (3%)
    pallas_call x1, Pallas kernels, per_device(): pl.pallas_call(functools.partial(kernel, nb, nu, n, fc), out_shape=(out,...  93.3 us
    unnamed x2, local copies, waits for them, and re-layouts  2.95 us

profile of v1, /device:TPU:0, one launch (start us, length us, event | category | flops | bytes accessed | tf_op | source)
XLA Modules:
  0.0 96.9 jit_solution(6181639450444675325)
XLA Ops:
  0.6 93.3 %shard_map.68 = (bf16[10,2048]{1,0:T(8,128)(2,1)}, bf16[10,2048]{1,0:T(8,128)(2,1)}) custom-call(bf16[10,2048]{1,0:T(8,128)(2,1)} %tok_in.1, bf16[10,2048]{1,0:T(8,128)(2,1)} %cot_in.1, bf16[2048,6656]{1,0:T(8,128)(2,1)} %wg_hbm.1, bf16[2048,6656]{1,0:T(8,128)(2,1)} %wu_hbm.1, bf16[6656,2048]{1,0:T(8,128)(2,1)} %wd_hbm.1), custom_call_target="tpu_custom_call" | custom-call | tf_op jit(solution)/shard_map/pallas_call | solution.py:311
  94.0 1.5 %copy.9 = bf16[10,2048]{1,0:T(8,128)(2,1)} copy(bf16[10,2048]{1,0:T(8,128)(2,1)} %get-tuple-element.4) | data formatting | bytes 81920
  95.5 1.5 %copy.10 = bf16[10,2048]{1,0:T(8,128)(2,1)} copy(bf16[10,2048]{1,0:T(8,128)(2,1)} %get-tuple-element.5) | data formatting | bytes 81920

commit v2 on v1

--- a/solution.py
+++ b/solution.py
@@ -11,21 +11,21 @@
 BF = jnp.bfloat16
 F32 = jnp.float32
 
-S1 = 1
-S2 = 3
-S3 = 4
-S4 = 7
-S5 = 8
-S6 = 11
-AHEAD = 8
+AHEAD = 12
 RING = 3
+LAG = 6
+def lags(n):
+    return (1, 3, 5, 9, 10, 15) if n >= 24 else (1, 3, 4, 7, 8, 11)
+
+
 NT = (((1,), (1,)), ((), ()))
 
 
-def kernel(nb, nu, n, fc, tok_in, cot_in, wg_hbm, wu_hbm, wd_hbm, mixed_out, grad_out,
-           wg, wu, wd, tok_g, cot_g, tok, cot, part, pair, far, act, mixed, grad, stage, zbuf,
+def kernel(nb, nu, n, fc, tok_in, cot_in, wg_hbm, wu_hbm, wd_hbm, out,
+           wg, wu, wd, tok_g, cot_g, tok, cot, part, pair, chip, far, act, mixed, grad, stage, zbuf,
            g_sem, u_sem, d_sem, tk_send, tk_recv, p_send, p_recv, f_send, f_recv,
            a_send, a_recv, fw_send, z_send, z_recv):
+    S1, S2, S3, S4, S5, S6 = lags(n)
     b_me = lax.axis_index("blk")
     u_me = lax.axis_index("bulk")
     x_me, k_me = u_me // 2, u_me % 2
@@ -40,12 +40,16 @@
                 pltpu.make_async_copy(wu_hbm.at[:, cols], wu.at[c], u_sem.at[c]))
 
     def load_d(m):
-        c = m % n
-        slot = m % RING
+        m = jnp.int32(m)
+        c = lax.rem(m, n)
+        slot = lax.rem(m, RING)
         return pltpu.make_async_copy(
             wd_hbm.at[pl.ds(pl.multiple_of(c * fc, fc), fc), :], wd.at[slot], d_sem.at[slot])
 
     ahead = min(AHEAD, n)
+    lag = min(LAG, n - S6)
+    keep = part.shape[0]
+    many = 2 if n % 2 == 0 else 1
     for c in range(ahead):
         for cp in load_gu(c):
             cp.start()
@@ -71,9 +75,11 @@
     for w in range(2):
         for d in range(1, nb):
             tok_copy(w, d).start()
-    for src, got, dst, which in ((tok_in, tok_g, tok, 0), (cot_in, cot_g, cot, 1)):
-        for d in range(1, nb):
-            tok_copy(which, d).wait_recv()
+
+    def gather(w):
+        src, got, dst = (tok_in, tok_g, tok) if w == 0 else (cot_in, cot_g, cot)
+        for d in range(1, nb):
+            tok_copy(w, d).wait_recv()
         for h in range(2):
             cols = pl.ds(h * dh, dh)
             for b in range(nb):
@@ -85,28 +91,28 @@
             dst[:, h * dh:(h + 1) * dh] = mixed[h].astype(BF)
 
     def owner(c):
-        o = c % nu
-        return o, o // 2, o % 2
+        o = lax.rem(c, nu)
+        return o, lax.div(o, 2), lax.rem(o, 2)
 
     def pair_copy(c):
-        return rcopy(part.at[c], pair.at[c // 2], p_send.at[c], p_recv.at[c // 2], {"bulk": partner})
+        return rcopy(part.at[lax.rem(c, keep)], pair.at[lax.div(c, 2)], p_send.at[c], p_recv.at[lax.div(c, 2)], {"bulk": partner})
 
     def far_copy(c):
         o, ox, ok = owner(c)
         slot = (x_me - ox + chips - 1 + chips) % chips
-        return rcopy(pair.at[c // 2], far.at[c // nu, slot], f_send.at[c // 2],
-                     f_recv.at[c // nu, slot], {"bulk": o})
+        return rcopy(chip.at[lax.div(c, 2)], far.at[lax.div(c, nu), slot], f_send.at[lax.div(c, 2)],
+                     f_recv.at[lax.div(c, nu), slot], {"bulk": o})
 
     def far_wait(c, slot):
-        rcopy(pair.at[c // 2], far.at[c // nu, slot], f_send.at[c // 2],
-              f_recv.at[c // nu, slot], {"bulk": partner}).wait_recv()
+        rcopy(chip.at[lax.div(c, 2)], far.at[lax.div(c, nu), slot], f_send.at[lax.div(c, 2)],
+              f_recv.at[lax.div(c, nu), slot], {"bulk": partner}).wait_recv()
 
     def act_copy(c, d):
         to = partner if d == 0 else ((x_me + d) % chips) * 2 + k_me
-        return rcopy(act.at[c], act.at[c], a_send.at[c // nu, d], a_recv.at[c], {"bulk": to})
+        return rcopy(act.at[c], act.at[c], a_send.at[lax.div(c, nu), d], a_recv.at[c], {"bulk": to})
 
     def forward(c):
-        return rcopy(act.at[c], act.at[c], fw_send.at[c // 2], a_recv.at[c], {"bulk": partner})
+        return rcopy(act.at[c], act.at[c], fw_send.at[lax.div(c, 2)], a_recv.at[c], {"bulk": partner})
 
     def valid(c):
         return jnp.logical_and(c >= 0, c < n)
@@ -150,10 +156,14 @@
             @pl.when(o2[1] != x_me)
             def _():
                 for j in range(3):
-                    pair[c2 // 2, j] = (
-                        part[c2, j].astype(F32) + pair[c2 // 2, j].astype(F32)).astype(BF)
+                    chip[lax.div(c2, 2), j] = (
+                        part[lax.rem(c2, keep), j] + pair[lax.div(c2, 2), j]).astype(BF)
 
         c4 = i - S4
+
+        @pl.when(jnp.logical_and(valid(c4), owner(c4 + nu)[2] != k_me))
+        def _():
+            pair_copy(c4).wait_send()
 
         @pl.when(jnp.logical_and(valid(c4), owner(c4 + nu)[0] == u_me))
         def _():
@@ -161,9 +171,9 @@
                 far_wait(c4, slot)
 
             def total(j):
-                s = part[c4, j].astype(F32) + pair[c4 // 2, j].astype(F32)
+                s = part[lax.rem(c4, keep), j] + pair[lax.div(c4, 2), j]
                 for slot in range(chips - 1):
-                    s = s + far[c4 // nu, slot, j].astype(F32)
+                    s = s + far[lax.div(c4, nu), slot, j].astype(F32)
                 return s
 
             gate, upward, back = total(0), total(1), total(2)
@@ -172,45 +182,61 @@
             act[c4, 1] = (back * upward * sigma * (1.0 + gate * (1.0 - sigma))).astype(BF)
             act[c4, 2] = (back * gate * sigma).astype(BF)
 
-    def first(i, _):
-        stages(i)
-
-        @pl.when(i + ahead < n)
-        def _():
-            for cp in load_gu(i + ahead):
-                cp.start()
-
-        for cp in load_gu(i):
-            cp.wait()
-        part[i, 0] = jnp.dot(tok[...], wg[i], preferred_element_type=F32).astype(BF)
-        part[i, 1] = jnp.dot(tok[...], wu[i], preferred_element_type=F32).astype(BF)
-        load_d(i).wait()
-        part[i, 2] = lax.dot_general(
-            cot[...], wd[i % RING], NT, preferred_element_type=F32).astype(BF)
-        load_d(i + RING).start()
+    def first(gu, back, i, _):
+        m = i - lag
+        stages(m)
+        if gu:
+            @pl.when(i + ahead < n)
+            def _():
+                for cp in load_gu(i + ahead):
+                    cp.start()
+
+            for cp in load_gu(i):
+                cp.wait()
+        if back:
+            load_d(m).wait()
+        if gu:
+            part[lax.rem(i, keep), 0] = jnp.dot(tok[...], wg[i], preferred_element_type=F32)
+            part[lax.rem(i, keep), 1] = jnp.dot(tok[...], wu[i], preferred_element_type=F32)
+        if back:
+            part[lax.rem(m, keep), 2] = lax.dot_general(
+                cot[...], wd[lax.rem(m, RING)], NT, preferred_element_type=F32)
+            load_d(m + RING).start()
         return 0
 
-    lax.fori_loop(0, n, first, 0)
+    gather(0)
+    lax.fori_loop(0, lag, functools.partial(first, True, False), 0)
+    gather(1)
+    lax.fori_loop(lag, n, functools.partial(first, True, True), 0)
+    lax.fori_loop(n, n + lag, functools.partial(first, False, True), 0)
 
     mixed[...] = jnp.zeros_like(mixed)
     grad[...] = jnp.zeros_like(grad)
 
+    def add_grad(h, c):
+        grad[h] += (
+            lax.dot_general(act[c, 1], wg[c, h * dh:(h + 1) * dh, :], NT,
+                            preferred_element_type=F32)
+            + lax.dot_general(act[c, 2], wu[c, h * dh:(h + 1) * dh, :], NT,
+                              preferred_element_type=F32))
+
     def second(j, _):
-        i = j + n
-        stages(i)
+        m = j + n
+        stages(m)
 
         @pl.when(owner(j)[2] != k_me)
         def _():
             forward(j).wait_recv()
 
-        load_d(i).wait()
+        load_d(m).wait()
+        add_grad(0, j)
         for h in range(2):
             mixed[h] += jnp.dot(
-                act[j, 0], wd[i % RING, :, h * dh:(h + 1) * dh], preferred_element_type=F32)
-
-        @pl.when(i + RING < 2 * n)
-        def _():
-            load_d(i + RING).start()
+                act[j, 0], wd[lax.rem(m, RING), :, h * dh:(h + 1) * dh], preferred_element_type=F32)
+
+        @pl.when(m + RING < 2 * n)
+        def _():
+            load_d(m + RING).start()
 
         return 0
 
@@ -231,7 +257,7 @@
             z_copy(q, d).start()
 
     def z_finish(q):
-        acc, out = (mixed, mixed_out) if q < 2 else (grad, grad_out)
+        acc = mixed if q < 2 else grad
         h = q % 2
         s = jnp.zeros((rows, dh), F32)
         for b in range(nb):
@@ -239,26 +265,23 @@
         for d in range(1, nb):
             z_copy(q, d).wait_recv()
             s = s + zbuf[q, d - 1].astype(F32)
-        out[:, h * dh:(h + 1) * dh] = s.astype(BF)
-
-    z_stage(0)
-    z_stage(1)
-    for h in range(2):
-        def third(c, _, h=h):
-            @pl.when(c == 1)
-            def _():
-                for q in ((0, 1) if h == 0 else (2,)):
-                    z_send_all(q)
-
-            grad[h] += (
-                lax.dot_general(act[c, 1], wg[c, h * dh:(h + 1) * dh, :], NT,
-                                preferred_element_type=F32)
-                + lax.dot_general(act[c, 2], wu[c, h * dh:(h + 1) * dh, :], NT,
-                                  preferred_element_type=F32))
-            return 0
-
-        lax.fori_loop(0, n, third, 0)
-        z_stage(2 + h)
+        out[q // 2, :, h * dh:(h + 1) * dh] = s
+
+    for q in range(3):
+        z_stage(q)
+
+    def third(c, _):
+        @pl.when(c == 1)
+        def _():
+            for q in range(3):
+                z_send_all(q)
+
+        for k in range(many):
+            add_grad(1, c * many + k)
+        return 0
+
+    lax.fori_loop(0, n // many, third, 0)
+    z_stage(3)
     z_finish(0)
     z_send_all(3)
     z_finish(1)
@@ -270,10 +293,6 @@
 
     def drain(c, _):
         o, ox, ok = owner(c)
-
-        @pl.when(ok != k_me)
-        def _():
-            pair_copy(c).wait_send()
 
         @pl.when(jnp.logical_and(ok == k_me, ox != x_me))
         def _():
@@ -299,6 +318,7 @@
     width = gate_weight.shape[1]
     fc = next(w for w in (256, 128) if width % w == 0)
     n = width // fc
+    S4, S6 = lags(n)[3], lags(n)[5]
     assert n >= S6 and depth % 256 == 0 and nu % 2 == 0
     t = rows * nb
     dh = depth // 2
@@ -307,17 +327,16 @@
     chips = nu // 2
     dma = pltpu.SemaphoreType.DMA
     vm = pltpu.VMEM
-    out = jax.ShapeDtypeStruct((rows, depth), BF)
-    return pl.pallas_call(
+    both = pl.pallas_call(
         functools.partial(kernel, nb, nu, n, fc),
-        out_shape=(out, out),
+        out_shape=jax.ShapeDtypeStruct((2, rows, depth), F32),
         in_specs=[pl.BlockSpec(memory_space=pltpu.VMEM)] * 2 + [pl.BlockSpec(memory_space=pl.ANY)] * 3,
-        out_specs=(pl.BlockSpec(memory_space=pltpu.VMEM),) * 2,
+        out_specs=pl.BlockSpec(memory_space=pltpu.VMEM),
         scratch_shapes=[
             vm((n, depth, fc), BF), vm((n, depth, fc), BF), vm((RING, fc, depth), BF),
             vm((nb - 1, rows, depth), BF), vm((nb - 1, rows, depth), BF),
             vm((t, depth), BF), vm((t, depth), BF),
-            vm((n, 3, t, fc), BF), vm((halfn, 3, t, fc), BF), vm((owned, chips - 1, 3, t, fc), BF),
+            vm((S4 + min(LAG, n - S6), 3, t, fc), F32), vm((halfn, 3, t, fc), F32), vm((halfn, 3, t, fc), BF), vm((owned, chips - 1, 3, t, fc), BF),
             vm((n, 3, t, fc), BF),
             vm((2, t, dh), F32), vm((2, t, dh), F32),
             vm((4, nb, rows, dh), BF), vm((4, nb - 1, rows, dh), BF),
@@ -330,6 +349,7 @@
         compiler_params=pltpu.CompilerParams(
             collective_id=0, has_side_effects=True, vmem_limit_bytes=67043328),
     )(tokens, cotangent, gate_weight, up_weight, down_weight)
+    return both[0].astype(BF), both[1].astype(BF)
 
 
 def solution(mesh):

time: 97.3 us -> 83.1 us (0.85)
  Pallas kernels: 93.3 us -> 80.6 us
  local copies, waits for them, and re-layouts: 2.95 us -> 0.66 us
    pallas_call x1, Pallas kernels: 93.3 us -> 80.6 us  [per_device(): pl.pallas_call(functools.partial(kernel, nb, nu, n, fc), out_shape=jax.Sh...]
    unnamed x2 -> x0, local copies, waits for them, and re-layouts: 2.95 us -> none
where the time goes in v2:
time: 83.1 us; the launch traced here: 82.9 us
  Pallas kernels  80.6 us (97%)
  other arithmetic  0.97 us (1%)
    pallas_call x1, Pallas kernels, per_device(): pl.pallas_call(functools.partial(kernel, nb, nu, n, fc), out_shape=jax.Sh...  80.6 us

profile of v2, /device:TPU:0, one launch (start us, length us, event | category | flops | bytes accessed | tf_op | source)
XLA Modules:
  0.0 82.9 jit_solution(17970302446832173188)
XLA Ops:
  0.6 80.6 %shard_map.68 = f32[2,10,2048]{2,1,0:T(8,128)} custom-call(bf16[10,2048]{1,0:T(8,128)(2,1)} %tok_in.1, bf16[10,2048]{1,0:T(8,128)(2,1)} %cot_in.1, bf16[2048,6656]{1,0:T(8,128)(2,1)} %wg_hbm.1, bf16[2048,6656]{1,0:T(8,128)(2,1)} %wu_hbm.1, bf16[6656,2048]{1,0:T(8,128)(2,1)} %wd_hbm.1), custom_call_target="tpu_custom_call" | custom-call | tf_op jit(solution)/shard_map/pallas_call | solution.py:330
  81.2 1.0 %convert.4 = bf16[2,10,2048]{2,1,0:T(8,128)(2,1)S(1)} convert(f32[2,10,2048]{2,1,0:T(8,128)} %shard_map.68) | non-fusion elementwise | flops 40960 | bytes 245760 | tf_op jit(solution)/shard_map/convert.1
  82.2 0.7 slice_bitcast_fusion

commit v3 on v2

--- a/solution.py
+++ b/solution.py
@@ -11,9 +11,9 @@
 BF = jnp.bfloat16
 F32 = jnp.float32
 
-AHEAD = 12
+AHEAD = 20
 RING = 3
-LAG = 6
+LAG = 4
 def lags(n):
     return (1, 3, 5, 9, 10, 15) if n >= 24 else (1, 3, 4, 7, 8, 11)
 
@@ -22,7 +22,7 @@
 
 
 def kernel(nb, nu, n, fc, tok_in, cot_in, wg_hbm, wu_hbm, wd_hbm, out,
-           wg, wu, wd, tok_g, cot_g, tok, cot, part, pair, chip, far, act, mixed, grad, stage, zbuf,
+           wg, wu, wd, own, tok_g, cot_g, tok, cot, part, pair, chip, far, act, mixed, grad, stage, zbuf,
            g_sem, u_sem, d_sem, tk_send, tk_recv, p_send, p_recv, f_send, f_recv,
            a_send, a_recv, fw_send, z_send, z_recv):
     S1, S2, S3, S4, S5, S6 = lags(n)
@@ -56,6 +56,11 @@
         if c < RING:
             load_d(c).start()
 
+    own[...] = jnp.zeros_like(own)
+    own[0, :rows, :] = tok_in[...]
+    own[1, :rows, :] = cot_in[...]
+    stage[...] = jnp.zeros_like(stage)
+
     barrier = pltpu.get_barrier_semaphore()
     for d in range(1, nb):
         pl.semaphore_signal(barrier, inc=1, device_id={"blk": (b_me + d) % nb}, device_id_type=MESH)
@@ -68,8 +73,8 @@
             src_ref=src, dst_ref=dst, send_sem=ss, recv_sem=rs, device_id=where, device_id_type=MESH)
 
     def tok_copy(w, d):
-        src, dst = (tok_in, tok_g) if w == 0 else (cot_in, cot_g)
-        return rcopy(src, dst.at[d - 1], tk_send.at[w, d - 1], tk_recv.at[w, d - 1],
+        dst = tok_g if w == 0 else cot_g
+        return rcopy(own.at[w], dst.at[d - 1], tk_send.at[w, d - 1], tk_recv.at[w, d - 1],
                      {"blk": (b_me + d) % nb})
 
     for w in range(2):
@@ -84,9 +89,9 @@
             cols = pl.ds(h * dh, dh)
             for b in range(nb):
                 slot = (b_me - b + nb) % nb
-                other = got[jnp.maximum(slot - 1, 0), :, cols].astype(F32)
-                own = src[:, cols].astype(F32)
-                mixed[h, pl.ds(b * rows, rows), :] = jnp.where(slot == 0, own, other)
+                other = got[jnp.maximum(slot - 1, 0), :rows, cols].astype(F32)
+                mine = src[:, cols].astype(F32)
+                mixed[h, pl.ds(b * rows, rows), :] = jnp.where(slot == 0, mine, other)
         for h in range(2):
             dst[:, h * dh:(h + 1) * dh] = mixed[h].astype(BF)
 
@@ -245,7 +250,7 @@
     def z_stage(q):
         acc = mixed if q < 2 else grad
         for b in range(nb):
-            stage[q, b] = acc[q % 2, b * rows:(b + 1) * rows, :].astype(BF)
+            stage[q, b, :rows, :] = acc[q % 2, b * rows:(b + 1) * rows, :].astype(BF)
 
     def z_copy(q, d):
         to = (b_me + d) % nb
@@ -264,7 +269,7 @@
             s = s + jnp.where(b == b_me, acc[h, b * rows:(b + 1) * rows, :], 0.0)
         for d in range(1, nb):
             z_copy(q, d).wait_recv()
-            s = s + zbuf[q, d - 1].astype(F32)
+            s = s + zbuf[q, d - 1, :rows, :].astype(F32)
         out[q // 2, :, h * dh:(h + 1) * dh] = s
 
     for q in range(3):
@@ -321,6 +326,7 @@
     S4, S6 = lags(n)[3], lags(n)[5]
     assert n >= S6 and depth % 256 == 0 and nu % 2 == 0
     t = rows * nb
+    tile = pl.cdiv(rows, 16) * 16
     dh = depth // 2
     owned = pl.cdiv(n, nu)
     halfn = pl.cdiv(n, 2)
@@ -334,12 +340,12 @@
         out_specs=pl.BlockSpec(memory_space=pltpu.VMEM),
         scratch_shapes=[
             vm((n, depth, fc), BF), vm((n, depth, fc), BF), vm((RING, fc, depth), BF),
-            vm((nb - 1, rows, depth), BF), vm((nb - 1, rows, depth), BF),
+            vm((2, tile, depth), BF), vm((nb - 1, tile, depth), BF), vm((nb - 1, tile, depth), BF),
             vm((t, depth), BF), vm((t, depth), BF),
             vm((S4 + min(LAG, n - S6), 3, t, fc), F32), vm((halfn, 3, t, fc), F32), vm((halfn, 3, t, fc), BF), vm((owned, chips - 1, 3, t, fc), BF),
             vm((n, 3, t, fc), BF),
             vm((2, t, dh), F32), vm((2, t, dh), F32),
-            vm((4, nb, rows, dh), BF), vm((4, nb - 1, rows, dh), BF),
+            vm((4, nb, tile, dh), BF), vm((4, nb - 1, tile, dh), BF),
             dma((n,)), dma((n,)), dma((RING,)),
             dma((2, nb - 1)), dma((2, nb - 1)),
             dma((n,)), dma((halfn,)), dma((halfn,)), dma((owned, chips - 1)),

time: 83.1 us -> 82.1 us (0.988)
  Pallas kernels: 80.6 us -> 79.7 us
    pallas_call x1, Pallas kernels: 80.6 us -> 79.7 us  [per_device(): pl.pallas_call(functools.partial(kernel, nb, nu, n, fc), out_shape=jax.Sh...]
where the time goes in v3:
time: 82.1 us; the launch traced here: 81.9 us
  Pallas kernels  79.7 us (97%)
  other arithmetic  0.97 us (1%)
    pallas_call x1, Pallas kernels, per_device(): pl.pallas_call(functools.partial(kernel, nb, nu, n, fc), out_shape=jax.Sh...  79.7 us

profile of v3, /device:TPU:0, one launch (start us, length us, event | category | flops | bytes accessed | tf_op | source)
XLA Modules:
  0.0 81.9 jit_solution(8778509553507227638)
XLA Ops:
  0.6 79.7 %shard_map.68 = f32[2,10,2048]{2,1,0:T(8,128)} custom-call(bf16[10,2048]{1,0:T(8,128)(2,1)} %tok_in.1, bf16[10,2048]{1,0:T(8,128)(2,1)} %cot_in.1, bf16[2048,6656]{1,0:T(8,128)(2,1)} %wg_hbm.1, bf16[2048,6656]{1,0:T(8,128)(2,1)} %wu_hbm.1, bf16[6656,2048]{1,0:T(8,128)(2,1)} %wd_hbm.1), custom_call_target="tpu_custom_call" | custom-call | tf_op jit(solution)/shard_map/pallas_call | solution.py:336
  80.3 1.0 %convert.4 = bf16[2,10,2048]{2,1,0:T(8,128)(2,1)S(1)} convert(f32[2,10,2048]{2,1,0:T(8,128)} %shard_map.68) | non-fusion elementwise | flops 40960 | bytes 245760 | tf_op jit(solution)/shard_map/convert.1
  81.3 0.7 slice_bitcast_fusion
